TPU v7x, 1024 devices: a whole 8x8x8 slice. The times are simulated.
1024 devices in a mesh: ctx: 64 (over x, z), head: 16 (over y, core).
Axes of the slice: x: 8, y: 8, z: 8, core: 2. Of those that a mesh axis runs over, the one named last changes fastest.
Arguments:
- queries: bfloat16 [8192, 6144], P('ctx', 'head'), as said below
- key_rows: bfloat16 [8192, 6144], P('ctx', 'head')
- value_rows: bfloat16 [8192, 6144], P('ctx', 'head'), may hold values from -6 to 6
- summary_index: int32 [64], P('ctx'), may hold values from 0 to 15
- out_weight: bfloat16 [6144, 6144], P('head'), may hold values from -0.078125 to 0.078125
- out_grad: bfloat16 [8192, 6144], P('ctx'), may hold values from -6 to 6
Outputs:
- attended: bfloat16 [8192, 6144], P('ctx', 'head')
- grad_query: bfloat16 [8192, 6144], P('ctx', 'head')
- grad_key: bfloat16 [8192, 6144], P('ctx', 'head')
- grad_value: bfloat16 [8192, 6144], P('ctx', 'head')
Inputs may be any that keep to these rules, and one draw needn't show every extreme that they name: queries and keys are finite bfloat16 values.
All inputs are finite; a program needn't handle non-finite values.
Results may differ from a plain program's by a relative error of at most 0.018.
Values may be sent and summed in bfloat16 or wider, within the bound.
A program may use at most 32 MiB of HBM per device.

v0:
```python
import jax
import jax.numpy as jnp
from jax import lax
from jax.sharding import PartitionSpec as P

HEAD_DIM = 128
STRIDE = 128
SUMMARY = 8


def shifted(value, axis, steps):
    count = lax.axis_size(axis)
    leading, last = (max(0, -steps), min(count, count - steps))
    return lax.ppermute(value, axis, [(source, source + steps) for source in range(leading, last)])


def on_device(queries, key_rows, value_rows, summary_index, out_weight, out_grad):
    rows, width = queries.shape
    heads = width // HEAD_DIM
    shards = lax.axis_size("ctx")
    place = lax.axis_index("ctx")
    strides_here = rows // STRIDE
    blocks = STRIDE // SUMMARY
    per_shard = strides_here * SUMMARY
    slots = shards * per_shard
    scale = HEAD_DIM ** (-0.5)
    first = place * per_shard

    def pick(values):
        shaped = values.reshape(strides_here, blocks, SUMMARY, width)
        chosen = jnp.take_along_axis(shaped, summary_index.reshape(strides_here, 1, 1, 1), axis=1)
        return chosen.reshape(per_shard, width)

    own_keys = pick(key_rows)
    own_vals = pick(value_rows)
    blank = jnp.zeros((slots, width), jnp.bfloat16)
    start_keys = lax.dynamic_update_slice_in_dim(blank, own_keys, first, 0)
    start_vals = lax.dynamic_update_slice_in_dim(blank, own_vals, first, 0)

    def forward_turn(turn, state):
        table_keys, table_vals, moving_keys, moving_vals = state
        moving_keys, moving_vals = shifted((moving_keys, moving_vals), "ctx", 1)
        source = place - turn
        valid = source >= 0
        offset = jnp.maximum(source, 0) * per_shard
        old_keys = lax.dynamic_slice_in_dim(table_keys, offset, per_shard, 0)
        old_vals = lax.dynamic_slice_in_dim(table_vals, offset, per_shard, 0)
        table_keys = lax.dynamic_update_slice_in_dim(
            table_keys, jnp.where(valid, moving_keys, old_keys), offset, 0
        )
        table_vals = lax.dynamic_update_slice_in_dim(
            table_vals, jnp.where(valid, moving_vals, old_vals), offset, 0
        )
        return (table_keys, table_vals, moving_keys, moving_vals)

    all_keys, all_vals, unused_keys, unused_vals = lax.fori_loop(
        1, shards, forward_turn, (start_keys, start_vals, own_keys, own_vals)
    )
    dattn = lax.dot_general(
        out_grad, out_weight, (((1,), (1,)), ((), ())), preferred_element_type=jnp.float32
    ).astype(jnp.bfloat16)
    q_heads = queries.reshape(rows, heads, HEAD_DIM)
    k_heads = key_rows.reshape(rows, heads, HEAD_DIM)
    v_heads = value_rows.reshape(rows, heads, HEAD_DIM)
    sk_heads = all_keys.reshape(slots, heads, HEAD_DIM)
    sv_heads = all_vals.reshape(slots, heads, HEAD_DIM)
    da_heads = dattn.reshape(rows, heads, HEAD_DIM)
    positions = jnp.arange(rows)
    local_block = positions // STRIDE
    query_block = place * strides_here + local_block
    causal = (local_block[:, None] == local_block[None, :]) & (
        positions[:, None] >= positions[None, :]
    )
    visible = (jnp.arange(slots) // SUMMARY)[None, :] < query_block[:, None]
    s_loc = jnp.einsum("qhd,khd->hqk", q_heads, k_heads, preferred_element_type=jnp.float32) * scale
    s_loc = jnp.where(causal[None], s_loc, -jnp.inf)
    s_sum = (
        jnp.einsum("qhd,khd->hqk", q_heads, sk_heads, preferred_element_type=jnp.float32) * scale
    )
    s_sum = jnp.where(visible[None], s_sum, -jnp.inf)
    top = jnp.maximum(
        jnp.max(s_loc, axis=-1, keepdims=True), jnp.max(s_sum, axis=-1, keepdims=True)
    )
    e_loc = jnp.exp(s_loc - top)
    e_sum = jnp.exp(s_sum - top)
    total = jnp.sum(e_loc, axis=-1, keepdims=True) + jnp.sum(e_sum, axis=-1, keepdims=True)
    p_loc = e_loc / total
    p_sum = e_sum / total
    pb_loc = p_loc.astype(jnp.bfloat16)
    pb_sum = p_sum.astype(jnp.bfloat16)
    attn = (
        jnp.einsum("hqk,khd->qhd", pb_loc, v_heads, preferred_element_type=jnp.float32)
        + jnp.einsum("hqk,khd->qhd", pb_sum, sv_heads, preferred_element_type=jnp.float32)
    ).astype(jnp.bfloat16)
    partial_out = jnp.dot(attn.reshape(rows, width), out_weight, preferred_element_type=jnp.float32)
    attended = lax.psum_scatter(
        partial_out.astype(jnp.bfloat16), "head", scatter_dimension=1, tiled=True
    )
    dp_loc = jnp.einsum("qhd,khd->hqk", da_heads, v_heads, preferred_element_type=jnp.float32)
    dp_sum = jnp.einsum("qhd,khd->hqk", da_heads, sv_heads, preferred_element_type=jnp.float32)
    delta = jnp.sum(p_loc * dp_loc, axis=-1, keepdims=True) + jnp.sum(
        p_sum * dp_sum, axis=-1, keepdims=True
    )
    ds_loc = (p_loc * (dp_loc - delta)).astype(jnp.bfloat16)
    ds_sum = (p_sum * (dp_sum - delta)).astype(jnp.bfloat16)
    grad_query = (
        scale
        * (
            jnp.einsum("hqk,khd->qhd", ds_loc, k_heads, preferred_element_type=jnp.float32)
            + jnp.einsum("hqk,khd->qhd", ds_sum, sk_heads, preferred_element_type=jnp.float32)
        )
    ).astype(jnp.bfloat16)
    dk_local = scale * jnp.einsum(
        "hqk,qhd->khd", ds_loc, q_heads, preferred_element_type=jnp.float32
    )
    dv_local = jnp.einsum("hqk,qhd->khd", pb_loc, da_heads, preferred_element_type=jnp.float32)
    term_keys = (
        scale * jnp.einsum("hqk,qhd->khd", ds_sum, q_heads, preferred_element_type=jnp.float32)
    ).reshape(slots, width)
    term_vals = jnp.einsum(
        "hqk,qhd->khd", pb_sum, da_heads, preferred_element_type=jnp.float32
    ).reshape(slots, width)
    empty = jnp.zeros((per_shard, width), jnp.float32)

    def backward_turn(turn, state):
        carried_keys, carried_vals = shifted((state[0], state[1]), "ctx", -1)
        owner = place - shards + 1 + turn
        valid = owner >= 0
        offset = jnp.maximum(owner, 0) * per_shard
        add_keys = lax.dynamic_slice_in_dim(term_keys, offset, per_shard, 0)
        add_vals = lax.dynamic_slice_in_dim(term_vals, offset, per_shard, 0)
        return (
            carried_keys + jnp.where(valid, add_keys, 0.0),
            carried_vals + jnp.where(valid, add_vals, 0.0),
        )

    mine_keys, mine_vals = lax.fori_loop(0, shards, backward_turn, (empty, empty))
    onehot = (jnp.arange(blocks)[None, :] == summary_index[:, None]).astype(jnp.float32)

    def spread(values):
        placed = onehot[:, :, None, None] * values.reshape(strides_here, 1, SUMMARY, width)
        return placed.reshape(rows, width)

    grad_key = (dk_local.reshape(rows, width) + spread(mine_keys)).astype(jnp.bfloat16)
    grad_value = (dv_local.reshape(rows, width) + spread(mine_vals)).astype(jnp.bfloat16)
    return (attended, grad_query.reshape(rows, width), grad_key, grad_value)


def solution(mesh):
    return jax.shard_map(
        on_device,
        mesh=mesh,
        in_specs=(
            P("ctx", "head"),
            P("ctx", "head"),
            P("ctx", "head"),
            P("ctx"),
            P("head", None),
            P("ctx", None),
        ),
        out_specs=(P("ctx", "head"), P("ctx", "head"), P("ctx", "head"), P("ctx", "head")),
        check_vma=False,
    )
```

profile of v0, /device:TPU:104, one launch (start us, length us, event | category | flops | bytes accessed | tf_op | source)
XLA Modules:
  0.0 1482.4 jit_solution(8472333503295843656)
XLA Ops:
  12.7 691.8 %while.38 = (s32[]{:T(128)}, bf16[512,384]{1,0:T(8,128)(2,1)S(1)}, bf16[512,384]{1,0:T(8,128)(2,1)S(1)}, bf16[8,384]{1,0:T(8,128)(2,1)S(1)}, bf16[8,384]{1,0:T(8...) while((s32[]{:T(128)}, bf16[512,384]{1,0:T(8,128)(2,1)S(1)}, ...), condition=%wide.region_2.4_spmd, body=%wide.region_1.3_spmd.sunk | while | flops 6153 | bytes 110862 | solution.py:56
  23.1 8.5 collective-permute-done.1
  733.6 738.6 %while.39 = (s32[]{:T(128)}, f32[8,384]{1,0:T(8,128)S(1)}, f32[8,384]{1,0:T(8,128)S(1)}, s32[]{:T(128)}, f32[512,384]{1,0:T(8,128)S(1)}, /*index=5*/f32[512,384]...) while((s32[]{:T(128)}, f32[8,384]{1,0:T(8,128)S(1)}, f32[8,384]{1,0:T(8,128)S(1)}, ...), condition=%wide.region_10.12_spmd.clone, body=%wide.region_9.11_spmd.clone.sunk | while | flops 18442 | bytes 221465 | solution.py:137
  743.9 5.2 collective-permute-start.2
  767.1 5.2 collective-permute-start.2
  778.6 5.2 collective-permute-start.2
  790.2 5.2 collective-permute-start.2
  801.7 5.2 collective-permute-start.2
  813.3 5.2 collective-permute-start.2
  824.8 5.2 collective-permute-start.2
  836.4 5.2 collective-permute-start.2
  859.5 5.2 collective-permute-start.2
  871.1 5.2 collective-permute-start.2
  882.6 5.2 collective-permute-start.2
  894.2 5.2 collective-permute-start.2
  917.3 5.2 collective-permute-start.2
  928.8 5.2 collective-permute-start.2
  940.4 5.3 collective-permute-start.2
  952.0 5.2 collective-permute-start.2
  963.6 5.2 collective-permute-start.2
  975.1 5.2 collective-permute-start.2
  986.7 5.2 collective-permute-start.2
  998.2 5.2 collective-permute-start.2
  1021.3 5.2 collective-permute-start.2
  1032.9 5.2 collective-permute-start.2
  1044.4 5.3 collective-permute-start.2
  1056.1 5.2 collective-permute-start.2
  1067.6 5.2 collective-permute-start.2
  1079.2 5.2 collective-permute-start.2
  1090.7 5.2 collective-permute-start.2
  1102.3 5.2 collective-permute-start.2
  1125.4 5.2 collective-permute-start.2
  1137.0 5.2 collective-permute-start.2
  1148.5 5.3 collective-permute-start.2
  1160.1 5.2 collective-permute-start.2
  1171.7 5.2 collective-permute-start.2
  1183.2 5.2 collective-permute-start.2
  1194.8 5.2 collective-permute-start.2
  1206.4 5.2 collective-permute-start.2
  1229.5 5.2 collective-permute-start.2
  1241.0 5.2 collective-permute-start.2
  1252.6 5.3 collective-permute-start.2
  1264.2 5.2 collective-permute-start.2
  1275.8 5.2 collective-permute-start.2
  1287.3 5.2 collective-permute-start.2
  1298.9 5.2 collective-permute-start.2
  1414.4 5.2 collective-permute-start.2
  1449.1 5.2 collective-permute-start.2
  (1036 shorter events, 1217.1 us)
Async XLA Ops:
  7.2 1466.8 %reduce-scatter.4.cloned.1.call-start = ((), (), s32[]{:S(2)}) async-start(), calls=%async_computation.1 | async-start | bytes 1671168
  12.7 18.9 %collective-permute-start.1 = (bf16[8,384]{1,0:T(8,128)(2,1)S(1)}, bf16[8,384]{1,0:T(8,128)(2,1)S(1)}, u32[]{:S(2)}, u32[]{:S(2)}) collective-permute-start(bf16[8,384]{1,0:T(8,128)(2,1)S(1)} %get-tuple-element.461), channel_id=1, source_target_pairs={{0,16},{16,32},{32,48},{48,64},{64,80},{80,96},{96,112},{112,128},... | collective-permute-start | bytes 18440 | tf_op jit(solution)/shard_map/while/body/eval_jaxpr/ppermute | solution.py:14
  17.9 15.6 %collective-permute-start = (bf16[8,384]{1,0:T(8,128)(2,1)S(1)}, bf16[8,384]{1,0:T(8,128)(2,1)S(1)}, u32[]{:S(2)}, u32[]{:S(2)}) collective-permute-start(bf16[8,384]{1,0:T(8,128)(2,1)S(1)} %get-tuple-element.460), channel_id=1, source_target_pairs={{0,16},{16,32},{32,48},{48,64},{64,80},{80,96},{96,112},{112,128},... | collective-permute-start | bytes 18440 | tf_op jit(solution)/shard_map/while/body/eval_jaxpr/ppermute | solution.py:14
  33.5 8.8 collective-permute-start.1
  35.5 8.8 collective-permute-start
  44.3 8.8 collective-permute-start.1
  46.3 8.8 collective-permute-start
  55.2 8.8 collective-permute-start.1
  66.0 8.8 collective-permute-start.1
  67.9 8.8 collective-permute-start
  76.8 8.8 collective-permute-start.1
  78.7 8.8 collective-permute-start
  87.6 8.8 collective-permute-start.1
  89.5 8.9 collective-permute-start
  98.5 8.8 collective-permute-start.1
  100.4 8.8 collective-permute-start
  109.3 8.8 collective-permute-start.1
  120.1 8.8 collective-permute-start.1
  122.0 8.8 collective-permute-start
  130.9 8.8 collective-permute-start.1
  132.9 8.8 collective-permute-start
  141.8 8.8 collective-permute-start.1
  143.7 8.8 collective-permute-start
  152.6 8.8 collective-permute-start.1
  154.5 8.8 collective-permute-start
  165.3 8.8 collective-permute-start
  174.2 8.8 collective-permute-start.1
  176.1 8.8 collective-permute-start
  185.0 8.8 collective-permute-start.1
  187.0 8.8 collective-permute-start
  195.8 8.9 collective-permute-start.1
  197.8 8.9 collective-permute-start
  206.7 8.8 collective-permute-start.1
  208.6 8.8 collective-permute-start
  217.5 8.8 collective-permute-start.1
  219.4 8.8 collective-permute-start
  239.1 8.8 collective-permute-start.1
  241.1 8.8 collective-permute-start
  250.0 8.8 collective-permute-start.1
  251.9 8.8 collective-permute-start
  260.8 8.8 collective-permute-start.1
  262.7 8.8 collective-permute-start
  273.5 8.9 collective-permute-start
  379.8 8.9 collective-permute-start.1
  381.7 8.9 collective-permute-start
  457.5 8.9 collective-permute-start
  563.8 8.9 collective-permute-start.1
  565.7 8.9 collective-permute-start
  (214 other events, 3664.1 us)
Sparse Core Ops, SparseCore 0:
  713.3 53.3 reduce-scatter.3
where the time goes:
time: 1500 us; the launch traced here: 1480 us
  starting transfers between devices  705 us (47%)
  waiting for transfers between devices  670 us (45%)
  other arithmetic  53.7 us (4%)
  local copies, waits for them, and re-layouts  17.1 us (1%)
  matrix products  15.2 us (1%)
  between operations  15.1 us (1%)
    ppermute x254, starting transfers between devices, shifted(): lax.ppermute(value, axis, [(source, source + steps) for source in range(l...  705 us
    ppermute x254, waiting for transfers between devices, shifted(): lax.ppermute(value, axis, [(source, source + steps) for source in range(l...  670 us
    add x64, other arithmetic, backward_turn(): carried_vals + jnp.where(valid, add_vals, 0.0)  45.6 us
  transfers between devices with their start and end apart: 255, of which 190 were waited for; matrix products, arithmetic and copies ran while one was open for 5% of the time, Pallas kernels for 0%

commit v1 on v0

v1 whole, which is shorter than its diff:
```python
import functools

import jax
import jax.numpy as jnp
from jax import lax
from jax.experimental import pallas as pl
from jax.experimental.pallas import tpu as pltpu
from jax.sharding import PartitionSpec as P

HEAD_DIM = 128
SUMMARY = 8
SIZES = (8, 8, 8, 2)
MESH = pl.DeviceIdType.MESH
F32 = jnp.float32
BF16 = jnp.bfloat16
NT = (((1,), (1,)), ((), ()))
TN = (((0,), (0,)), ((), ()))
KA, KB, VA, VB, GK1, GK2, GV1, GV2 = range(8)


def dot(a, b, dims=(((1,), (0,)), ((), ()))):
    return lax.dot_general(a, b, dims, preferred_element_type=F32)


def kernel(sizes, idx_ref, q_ref, k_ref, v_ref, w_hbm, og_hbm,
           att_out, gq_out, gk_out, gv_out,
           w_v, og_v, tk, tv, sk, sv, da, attn, sloc, dploc, ploc, psum,
           ysend, yrecv, ysum, ring, kg, vg, rk, rv, s2k, s2v, r2k, r2v, dkl, dvl,
           load_sem, send_sem, recv_sem, psend_sem, precv_sem, rsend_sem, rrecv_sem):
    X, Z, Y, C = sizes
    N = Y * C
    rows, width = q_ref.shape
    heads = width // HEAD_DIM
    slots = X * Z * SUMMARY
    scale = HEAD_DIM ** (-0.5)
    ctx = lax.axis_index("ctx")
    head = lax.axis_index("head")
    mx, mz = ctx // Z, ctx % Z
    my, mc = head // C, head % C

    def at_x(d):
        return (((mx + d) % X) * Z + mz, head)

    def at_z(d):
        return (mx * Z + (mz + d) % Z, head)

    def at_y(d):
        return (ctx, ((my + Y + d) % Y) * C + mc)

    partner = (ctx, my * C + (1 - mc))

    def load_w(n):
        return pltpu.make_async_copy(w_hbm.at[:, pl.ds(n * width, width)], w_v.at[n], load_sem.at[0, n])

    def load_g(n):
        return pltpu.make_async_copy(og_hbm.at[:, pl.ds(n * width, width)], og_v.at[n], load_sem.at[1, n])

    for n in range(N):
        load_g(n).start()
        load_w(n).start()

    barrier = pltpu.get_barrier_semaphore()

    def greet(device):
        pl.semaphore_signal(barrier, inc=1, device_id=device, device_id_type=MESH)

    @pl.loop(1, X)
    def _(d):
        greet(at_x(d))

    @pl.loop(1, Z)
    def _(d):
        greet(at_z(d))

    greet(partner)
    greet(at_y(1))
    greet(at_y(-1))

    blocks = rows // SUMMARY
    index = idx_ref[0]
    chosen = lax.broadcasted_iota(jnp.int32, (blocks, SUMMARY, width), 0) == index

    def pick(ref):
        shaped = ref[...].astype(F32).reshape(blocks, SUMMARY, width)
        return jnp.sum(jnp.where(chosen, shaped, 0.0), axis=0).astype(BF16)

    tk[mx, mz] = pick(k_ref)
    tv[mx, mz] = pick(v_ref)
    pl.semaphore_wait(barrier, (X - 1) + (Z - 1) + 3)

    def copy(src, dst, phase, d, device):
        return pltpu.make_async_remote_copy(
            src_ref=src, dst_ref=dst, send_sem=send_sem.at[phase, d], recv_sem=recv_sem.at[phase, d],
            device_id=device, device_id_type=MESH)

    def ka(d):
        return copy(tk.at[mx, mz], tk.at[mx, mz], KA, d, at_z(d))

    def va(d):
        return copy(tv.at[mx, mz], tv.at[mx, mz], VA, d, at_x(d))

    def kb(d):
        return copy(tk.at[mx], tk.at[mx], KB, d, at_x(d))

    def vb(d):
        return copy(tv.at[:, mz], tv.at[:, mz], VB, d, at_z(d))

    def gk1(d):
        return copy(kg.at[(mx + d) % X], rk.at[mx], GK1, d, at_x(d))

    def gv1(d):
        return copy(vg.at[:, (mz + d) % Z], rv.at[mz], GV1, d, at_z(d))

    def gk2(d):
        return copy(s2k.at[(mz + d) % Z], r2k.at[mz], GK2, d, at_z(d))

    def gv2(d):
        return copy(s2v.at[(mx + d) % X], r2v.at[mx], GV2, d, at_x(d))

    def start(make, count):
        @pl.loop(1, count)
        def _(d):
            make(d).start()

    def arrive(make, count):
        @pl.loop(1, count)
        def _(d):
            make(d).wait_recv()

    def sent(make, count):
        @pl.loop(1, count)
        def _(d):
            make(d).wait_send()

    start(ka, Z)
    start(va, X)

    total = jnp.zeros((rows, width), F32)
    for n in range(N):
        load_g(n).wait()
        load_w(n).wait()
        total += dot(og_v[n], w_v[n], NT)
    da[...] = total.astype(BF16)

    arrive(ka, Z)
    start(kb, X)
    arrive(va, X)
    start(vb, Z)

    causal = (lax.broadcasted_iota(jnp.int32, (rows, rows), 0)
              >= lax.broadcasted_iota(jnp.int32, (rows, rows), 1))
    cols = [slice(h * HEAD_DIM, (h + 1) * HEAD_DIM) for h in range(heads)]
    for h in range(heads):
        sloc[h] = jnp.where(causal, dot(q_ref[:, cols[h]], k_ref[:, cols[h]], NT) * scale, -jnp.inf)
        dploc[h] = dot(da[:, cols[h]], v_ref[:, cols[h]], NT)

    arrive(kb, X)
    sk[...] = tk[...].astype(F32).reshape(slots, width).astype(BF16)
    arrive(vb, Z)
    sv[...] = tv[...].astype(F32).reshape(slots, width).astype(BF16)

    visible = lax.broadcasted_iota(jnp.int32, (rows, slots), 1) < ctx * SUMMARY
    for h in range(heads):
        s_loc = sloc[h]
        s_sum = jnp.where(visible, dot(q_ref[:, cols[h]], sk[:, cols[h]], NT) * scale, -jnp.inf)
        top = jnp.maximum(jnp.max(s_loc, axis=-1, keepdims=True), jnp.max(s_sum, axis=-1, keepdims=True))
        e_loc = jnp.exp(s_loc - top)
        e_sum = jnp.exp(s_sum - top)
        norm = jnp.sum(e_loc, axis=-1, keepdims=True) + jnp.sum(e_sum, axis=-1, keepdims=True)
        inverse = 1.0 / norm
        p_loc = e_loc * inverse
        p_sum = e_sum * inverse
        ploc[h] = p_loc
        psum[h] = p_sum
        attn[:, cols[h]] = (dot(p_loc.astype(BF16), v_ref[:, cols[h]])
                            + dot(p_sum.astype(BF16), sv[:, cols[h]])).astype(BF16)

    def pair(i):
        return pltpu.make_async_remote_copy(
            src_ref=ysend.at[i], dst_ref=yrecv.at[i], send_sem=psend_sem.at[i], recv_sem=precv_sem.at[i],
            device_id=partner, device_id_type=MESH)

    far = Y // 2

    def nth(i):
        return (my + far + i) % Y

    @pl.loop(0, Y)
    def _(i):
        to = nth(i)
        ysend[to] = dot(attn[...], w_v[to * C + (1 - mc)]).astype(BF16)
        pair(to).start()

    for h in range(heads):
        p_loc, p_sum = ploc[h], psum[h]
        da_h = da[:, cols[h]]
        q_h = q_ref[:, cols[h]]
        dp_loc = dploc[h]
        dp_sum = dot(da_h, sv[:, cols[h]], NT)
        delta = (jnp.sum(p_loc * dp_loc, axis=-1, keepdims=True)
                 + jnp.sum(p_sum * dp_sum, axis=-1, keepdims=True))
        ds_loc = (p_loc * (dp_loc - delta)).astype(BF16)
        ds_sum = (p_sum * (dp_sum - delta)).astype(BF16)
        kg[:, :, :, cols[h]] = (dot(ds_sum, q_h, TN) * scale).reshape(X, Z, SUMMARY, HEAD_DIM).astype(BF16)
        vg[:, :, :, cols[h]] = dot(p_sum.astype(BF16), da_h, TN).reshape(X, Z, SUMMARY, HEAD_DIM).astype(BF16)
        gq_out[:, cols[h]] = (scale * (dot(ds_loc, k_ref[:, cols[h]]) + dot(ds_sum, sk[:, cols[h]]))).astype(BF16)
        dkl[:, cols[h]] = scale * dot(ds_loc, q_h, TN)
        dvl[:, cols[h]] = dot(p_loc.astype(BF16), da_h, TN)

    start(gk1, X)
    start(gv1, Z)

    half = rows // 2
    chains = []
    for chunk in range(2):
        for way in (1, -1):
            hops = far if (chunk == 0) == (way == 1) else Y - 1 - far
            if hops:
                chains.append((chunk, way, hops))

    def hop(c, s):
        chunk, way, hops = chains[c]
        place = pl.ds(chunk * half, half)
        src = ysum.at[(my + Y + way * hops) % Y, place] if s == 0 else ring.at[c, s - 1]
        return pltpu.make_async_remote_copy(
            src_ref=src, dst_ref=ring.at[c, s], send_sem=rsend_sem.at[c, s], recv_sem=rrecv_sem.at[c, s],
            device_id=at_y(way), device_id_type=MESH)

    @pl.loop(0, Y)
    def _(i):
        to = nth(i)
        own = dot(attn[...], w_v[to * C + mc])
        pair(to).wait_recv()
        ysum[to] = (own + yrecv[to].astype(F32)).astype(BF16)

    for c in range(len(chains)):
        hop(c, 0).start()

    def relay(s):
        for c, (chunk, way, hops) in enumerate(chains):
            if s < hops:
                hop(c, s - 1).wait_recv()
                own = ysum[(my + Y + way * (hops - s)) % Y, chunk * half:(chunk + 1) * half]
                ring[c, s - 1] = (ring[c, s - 1].astype(F32) + own.astype(F32)).astype(BF16)
                hop(c, s).start()

    for s in range(1, far - 1):
        relay(s)

    arrive(gk1, X)

    def gathered(own, received, place, count):
        return lax.fori_loop(
            1, count, lambda d, acc: acc + received[(place + d) % count].astype(F32), own.astype(F32))

    s2k[...] = gathered(kg[mx], rk, mx, X).astype(BF16)
    start(gk2, Z)
    arrive(gv1, Z)
    s2v[...] = gathered(vg[:, mz], rv, mz, Z).astype(BF16)
    start(gv2, X)

    if far > 1:
        relay(far - 1)

    here = lax.broadcasted_iota(jnp.int32, (blocks, SUMMARY, width), 0) == index

    def spread(local, extra):
        shaped = local.reshape(blocks, SUMMARY, width)
        return jnp.where(here, shaped + extra[None], shaped).reshape(rows, width).astype(BF16)

    arrive(gk2, Z)
    gk_out[...] = spread(dkl[...], gathered(s2k[mz], r2k, mz, Z))
    arrive(gv2, X)
    gv_out[...] = spread(dvl[...], gathered(s2v[mx], r2v, mx, X))

    for chunk in range(2):
        place = slice(chunk * half, (chunk + 1) * half)
        value = ysum[my, place].astype(F32)
        for c, (which, way, hops) in enumerate(chains):
            if which == chunk:
                hop(c, hops - 1).wait_recv()
                value += ring[c, hops - 1].astype(F32)
        att_out[place, :] = value.astype(BF16)

    for make, count in ((ka, Z), (va, X), (kb, X), (vb, Z), (gk1, X), (gv1, Z), (gk2, Z), (gv2, X)):
        sent(make, count)

    @pl.loop(0, Y)
    def _(i):
        pair(i).wait_send()

    for c, (chunk, way, hops) in enumerate(chains):
        for s in range(hops):
            hop(c, s).wait_send()


def on_device(sizes, queries, key_rows, value_rows, summary_index, out_weight, out_grad):
    X, Z, Y, C = sizes
    rows, width = queries.shape
    heads = width // HEAD_DIM
    slots = X * Z * SUMMARY
    N = Y * C
    vmem = pl.BlockSpec(memory_space=pltpu.VMEM)
    hbm = pl.BlockSpec(memory_space=pl.ANY)
    out = jax.ShapeDtypeStruct((rows, width), BF16)
    table = (X, Z, SUMMARY, width)
    far = max(Y // 2, 1)
    scratch = [
        pltpu.VMEM((N, width, width), BF16),
        pltpu.VMEM((N, rows, width), BF16),
        pltpu.VMEM(table, BF16),
        pltpu.VMEM(table, BF16),
        pltpu.VMEM((slots, width), BF16),
        pltpu.VMEM((slots, width), BF16),
        pltpu.VMEM((rows, width), BF16),
        pltpu.VMEM((rows, width), BF16),
        pltpu.VMEM((heads, rows, rows), F32),
        pltpu.VMEM((heads, rows, rows), F32),
        pltpu.VMEM((heads, rows, rows), F32),
        pltpu.VMEM((heads, rows, slots), F32),
        pltpu.VMEM((Y, rows, width), BF16),
        pltpu.VMEM((Y, rows, width), BF16),
        pltpu.VMEM((Y, rows, width), BF16),
        pltpu.VMEM((4, far, rows // 2, width), BF16),
        pltpu.VMEM(table, BF16),
        pltpu.VMEM(table, BF16),
        pltpu.VMEM((X, Z, SUMMARY, width), BF16),
        pltpu.VMEM((Z, X, SUMMARY, width), BF16),
        pltpu.VMEM((Z, SUMMARY, width), BF16),
        pltpu.VMEM((X, SUMMARY, width), BF16),
        pltpu.VMEM((Z, SUMMARY, width), BF16),
        pltpu.VMEM((X, SUMMARY, width), BF16),
        pltpu.VMEM((rows, width), F32),
        pltpu.VMEM((rows, width), F32),
        pltpu.SemaphoreType.DMA((2, N)),
        pltpu.SemaphoreType.DMA((8, max(X, Z))),
        pltpu.SemaphoreType.DMA((8, max(X, Z))),
        pltpu.SemaphoreType.DMA((Y,)),
        pltpu.SemaphoreType.DMA((Y,)),
        pltpu.SemaphoreType.DMA((4, far)),
        pltpu.SemaphoreType.DMA((4, far)),
    ]
    return tuple(pl.pallas_call(
        functools.partial(kernel, sizes),
        out_shape=(out, out, out, out),
        in_specs=[pl.BlockSpec(memory_space=pltpu.SMEM), vmem, vmem, vmem, hbm, hbm],
        out_specs=(vmem, vmem, vmem, vmem),
        scratch_shapes=scratch,
        compiler_params=pltpu.CompilerParams(collective_id=0, has_side_effects=True),
        name="sparse_attention_step",
    )(summary_index, queries, key_rows, value_rows, out_weight, out_grad))


def solution(mesh, sizes=SIZES):
    return jax.shard_map(
        functools.partial(on_device, sizes),
        mesh=mesh,
        in_specs=(
            P("ctx", "head"),
            P("ctx", "head"),
            P("ctx", "head"),
            P("ctx"),
            P("head", None),
            P("ctx", None),
        ),
        out_specs=(P("ctx", "head"), P("ctx", "head"), P("ctx", "head"), P("ctx", "head")),
        check_vma=False,
    )
```

time: 1500 us -> 71.1 us (0.05)
  the two profiles are of different devices: /device:TPU:104 before, /device:TPU:16 now
where the time goes in v1:
time: 71.1 us; the launch traced here: 70.8 us
  Pallas kernels  63.3 us (89%)
  local copies, waits for them, and re-layouts  6.17 us (9%)
  between operations  1.29 us (2%)
    pallas_call x1, Pallas kernels, on_device(): pl.pallas_call(functools.partial(kernel, sizes), out_shape=(out, out, out...  63.3 us
    unnamed x4, local copies, waits for them, and re-layouts  6.17 us

profile of v1, /device:TPU:16, one launch (start us, length us, event | category | flops | bytes accessed | tf_op | source)
XLA Modules:
  0.0 70.8 jit_solution(16498050200660524451)
XLA Ops:
  1.3 63.3 %sparse_attention_step.1 = (bf16[128,384]{1,0:T(8,128)(2,1)}, bf16[128,384]{1,0:T(8,128)(2,1)}, bf16[128,384]{1,0:T(8,128)(2,1)}, bf16[128,384]{1,0:T(8,128)(2,1)}) custom-call(s32[1]{0:T(128)S(6)} %copy.14.idx_ref, bf16[128,384]{1,0:T(8,128)(2,1)} %q_ref.1, bf16[128,384]{1,0:T(8,128)(2,1)} %k_ref.1, bf16[128,384]{1,0:T(8,128)(2,1)} %v_ref.1, ...), custom_call_target="tpu_custom_call" | custom-call | tf_op jit(solution)/shard_map/sparse_attention_step/pallas_call | solution.py:343
  64.6 1.5 %copy.15 = bf16[128,384]{1,0:T(8,128)(2,1)} copy(bf16[128,384]{1,0:T(8,128)(2,1)} %get-tuple-element.8) | data formatting | bytes 196608
  66.1 1.5 %copy.16 = bf16[128,384]{1,0:T(8,128)(2,1)} copy(bf16[128,384]{1,0:T(8,128)(2,1)} %get-tuple-element.9) | data formatting | bytes 196608
  67.7 1.5 %copy.17 = bf16[128,384]{1,0:T(8,128)(2,1)} copy(bf16[128,384]{1,0:T(8,128)(2,1)} %get-tuple-element.10) | data formatting | bytes 196608
  69.2 1.5 %copy.18 = bf16[128,384]{1,0:T(8,128)(2,1)} copy(bf16[128,384]{1,0:T(8,128)(2,1)} %get-tuple-element.11) | data formatting | bytes 196608

commit v2 on v1

v2 whole, which is shorter than its diff:
```python
import functools

import jax
import jax.numpy as jnp
from jax import lax
from jax.experimental import pallas as pl
from jax.experimental.pallas import tpu as pltpu
from jax.sharding import PartitionSpec as P

HEAD_DIM = 128
SUMMARY = 8
CHUNKS = 4
SIZES = (8, 8, 8, 2)
MESH = pl.DeviceIdType.MESH
F32 = jnp.float32
BF16 = jnp.bfloat16
NT = (((1,), (1,)), ((), ()))
TN = (((0,), (0,)), ((), ()))
KA, VA, GK2, GV2 = range(4)


def dot(a, b, dims=(((1,), (0,)), ((), ()))):
    return lax.dot_general(a, b, dims, preferred_element_type=F32)


def kernel(sizes, idx_hbm, q_hbm, k_hbm, v_hbm, w_hbm, og_hbm,
           att_out, gq_out, gk_out, gv_out,
           idx_ref, q_ref, k_ref, v_ref, w_v, og_v, tk, tv, sk, da, attn, sloc, dploc, dsloc, pbloc, dssum,
           w_p, ysum, ring, kg, vg, rk, rv, s2k, s2v, r2k, r2v, dkl, dvl,
           load_sem, in_sem, send_sem, recv_sem, psend_sem, precv_sem, rsend_sem, rrecv_sem):
    X, Z, Y, C = sizes
    N = Y * C
    rows, width = q_ref.shape
    heads = width // HEAD_DIM
    slots = X * Z * SUMMARY
    scale = HEAD_DIM ** (-0.5)
    ctx = lax.axis_index("ctx")
    head = lax.axis_index("head")
    mx, mz = ctx // Z, ctx % Z
    my, mc = head // C, head % C

    def at_x(d):
        return (((mx + d) % X) * Z + mz, head)

    def at_z(d):
        return (mx * Z + (mz + d) % Z, head)

    def at_y(d):
        return (ctx, ((my + Y + d) % Y) * C + mc)

    partner = (ctx, my * C + (1 - mc))

    def load_w(n):
        return pltpu.make_async_copy(w_hbm.at[:, pl.ds(n * width, width)], w_v.at[n], load_sem.at[0, n])

    def load_g(n):
        return pltpu.make_async_copy(og_hbm.at[:, pl.ds(n * width, width)], og_v.at[n], load_sem.at[1, n])

    barrier = pltpu.get_barrier_semaphore()

    def greet(device):
        pl.semaphore_signal(barrier, inc=1, device_id=device, device_id_type=MESH)

    @pl.loop(1, X)
    def _(d):
        greet(at_x(d))

    @pl.loop(1, Z)
    def _(d):
        greet(at_z(d))

    greet(partner)
    greet(at_y(1))
    greet(at_y(-1))

    loads = [pltpu.make_async_copy(a, b, in_sem.at[i]) for i, (a, b) in enumerate(
        ((idx_hbm, idx_ref), (k_hbm, k_ref), (v_hbm, v_ref), (q_hbm, q_ref)))]
    for load in loads:
        load.start()

    @pl.loop(0, N)
    def _(n):
        load_g(n).start()
        load_w(n).start()

    for load in loads:
        load.wait()

    blocks = rows // SUMMARY
    index = idx_ref[0]
    cols = [slice(h * HEAD_DIM, (h + 1) * HEAD_DIM) for h in range(heads)]
    chosen = lax.broadcasted_iota(jnp.int32, (blocks, SUMMARY, HEAD_DIM), 0) == index

    def pick(ref, h):
        shaped = ref[:, cols[h]].astype(F32).reshape(blocks, SUMMARY, HEAD_DIM)
        return jnp.sum(jnp.where(chosen, shaped, 0.0), axis=0).astype(BF16)

    for h in range(heads):
        tk[h, mx, mz] = pick(k_ref, h)
        tv[h, mz, mx] = pick(v_ref, h)
    pl.semaphore_wait(barrier, (X - 1) + (Z - 1) + 3)

    def copy(src, dst, phase, d, device):
        return pltpu.make_async_remote_copy(
            src_ref=src, dst_ref=dst, send_sem=send_sem.at[phase, d], recv_sem=recv_sem.at[phase, d],
            device_id=device, device_id_type=MESH)

    KB1, VB1, GK1, GV1 = (4 + i * heads for i in range(4))

    def ka(d):
        return copy(tk.at[:, mx, mz], tk.at[:, mx, mz], KA, d, at_z(d))

    def va(d):
        return copy(tv.at[:, mz, mx], tv.at[:, mz, mx], VA, d, at_x(d))

    def kb(h):
        return lambda d: copy(tk.at[h, mx], tk.at[h, mx], KB1 + h, d, at_x(d))

    def vb(h):
        return lambda d: copy(tv.at[h, mz], tv.at[h, mz], VB1 + h, d, at_z(d))

    def gk1(h):
        return lambda d: copy(kg.at[h, (mx + d) % X], rk.at[h, mx], GK1 + h, d, at_x(d))

    def gv1(h):
        return lambda d: copy(vg.at[h, (mz + d) % Z], rv.at[h, mz], GV1 + h, d, at_z(d))

    def gk2(d):
        return copy(s2k.at[:, (mz + d) % Z], r2k.at[mz], GK2, d, at_z(d))

    def gv2(d):
        return copy(s2v.at[:, (mx + d) % X], r2v.at[mx], GV2, d, at_x(d))

    def start(make, count):
        @pl.loop(1, count)
        def _(d):
            make(d).start()

    def arrive(make, count):
        @pl.loop(1, count)
        def _(d):
            make(d).wait_recv()

    def sent(make, count):
        @pl.loop(1, count)
        def _(d):
            make(d).wait_send()

    def lend(i):
        return pltpu.make_async_remote_copy(
            src_ref=w_hbm.at[:, pl.ds((i * C + (1 - mc)) * width, width)], dst_ref=w_p.at[i],
            send_sem=psend_sem.at[i], recv_sem=precv_sem.at[i], device_id=partner, device_id_type=MESH)

    def share(h):
        return pltpu.make_async_remote_copy(
            src_ref=attn.at[:, pl.ds(h * HEAD_DIM, HEAD_DIM)],
            dst_ref=attn.at[:, pl.ds(width + h * HEAD_DIM, HEAD_DIM)],
            send_sem=psend_sem.at[Y + h], recv_sem=precv_sem.at[Y + h], device_id=partner, device_id_type=MESH)

    start(ka, Z)
    start(va, X)

    @pl.loop(0, Y)
    def _(i):
        lend(i).start()

    total = jnp.zeros((rows, width), F32)
    for n in range(N):
        load_g(n).wait()
        load_w(n).wait()
        total += dot(og_v[n], w_v[n], NT)
    da[...] = total.astype(BF16)

    arrive(ka, Z)
    start(kb(0), X)
    arrive(va, X)
    start(vb(0), Z)
    for h in range(1, heads):
        start(kb(h), X)
        start(vb(h), Z)

    causal = (lax.broadcasted_iota(jnp.int32, (rows, rows), 0)
              >= lax.broadcasted_iota(jnp.int32, (rows, rows), 1))
    for h in range(heads):
        sloc[h] = jnp.where(causal, dot(q_ref[:, cols[h]], k_ref[:, cols[h]], NT) * scale, -jnp.inf)
        dploc[h] = dot(da[:, cols[h]], v_ref[:, cols[h]], NT)

    visible = lax.broadcasted_iota(jnp.int32, (rows, slots), 1) < ctx * SUMMARY
    for h in range(heads):
        q_h, v_h, da_h = q_ref[:, cols[h]], v_ref[:, cols[h]], da[:, cols[h]]
        arrive(kb(h), X)
        sk[h] = tk[h].astype(F32).reshape(slots, HEAD_DIM).astype(BF16)
        s_loc = sloc[h]
        s_sum = jnp.where(visible, dot(q_h, sk[h], NT) * scale, -jnp.inf)
        top = jnp.maximum(jnp.max(s_loc, axis=-1, keepdims=True), jnp.max(s_sum, axis=-1, keepdims=True))
        e_loc = jnp.exp(s_loc - top)
        e_sum = jnp.exp(s_sum - top)
        norm = jnp.sum(e_loc, axis=-1, keepdims=True) + jnp.sum(e_sum, axis=-1, keepdims=True)
        inverse = 1.0 / norm
        p_loc = e_loc * inverse
        p_sum = e_sum * inverse
        arrive(vb(h), Z)
        sv_h = jnp.swapaxes(tv[h].astype(F32), 0, 1).reshape(slots, HEAD_DIM).astype(BF16)
        pb_loc, pb_sum = p_loc.astype(BF16), p_sum.astype(BF16)
        attn[:, cols[h]] = (dot(pb_loc, v_h) + dot(pb_sum, sv_h)).astype(BF16)
        share(h).start()
        dp_loc = dploc[h]
        dp_sum = dot(da_h, sv_h, NT)
        delta = (jnp.sum(p_loc * dp_loc, axis=-1, keepdims=True)
                 + jnp.sum(p_sum * dp_sum, axis=-1, keepdims=True))
        ds_sum = (p_sum * (dp_sum - delta)).astype(BF16)
        kg[h] = (dot(ds_sum, q_h, TN) * scale).reshape(X, Z, SUMMARY, HEAD_DIM).astype(BF16)
        vg[h] = jnp.swapaxes(dot(pb_sum, da_h, TN).reshape(X, Z, SUMMARY, HEAD_DIM), 0, 1).astype(BF16)
        start(gk1(h), X)
        start(gv1(h), Z)
        dsloc[h] = (p_loc * (dp_loc - delta)).astype(BF16)
        dssum[h] = ds_sum
        pbloc[h] = pb_loc

    far = Y // 2

    order = sorted(range(Y), key=lambda i: -min(i, Y - i))

    @pl.loop(0, Y)
    def _(i):
        lend(i).wait_recv()

    for h in range(heads):
        share(h).wait_recv()

    part = rows // CHUNKS
    chains = []
    for chunk in range(CHUNKS):
        for way in (1, -1):
            hops = far if (chunk % 2 == 0) == (way == 1) else Y - 1 - far
            if hops:
                chains.append((chunk, way, hops))

    def hop(c, s):
        chunk, way, hops = chains[c]
        place = pl.ds(chunk * part, part)
        src = ysum.at[(my + Y + way * hops) % Y, place] if s == 0 else ring.at[c, s - 1]
        return pltpu.make_async_remote_copy(
            src_ref=src, dst_ref=ring.at[c, s], send_sem=rsend_sem.at[c, s], recv_sem=rrecv_sem.at[c, s],
            device_id=at_y(way), device_id_type=MESH)

    def combine(i):
        to = (my + i) % Y
        own = dot(attn[:, :width], w_v[to * C + mc])
        ysum[to] = (own + dot(attn[:, width:], w_p[to])).astype(BF16)

    begun = set()
    for n, i in enumerate(order):
        combine(i)
        for c, (chunk, way, hops) in enumerate(chains):
            if c not in begun and (way * hops) % Y in order[:n + 1]:
                begun.add(c)
                hop(c, 0).start()

    def relay(s):
        for c, (chunk, way, hops) in enumerate(chains):
            if s < hops:
                hop(c, s - 1).wait_recv()
                own = ysum[(my + Y + way * (hops - s)) % Y, chunk * part:(chunk + 1) * part]
                ring[c, s - 1] = (ring[c, s - 1].astype(F32) + own.astype(F32)).astype(BF16)
                hop(c, s).start()

    def gathered(own, received, place, count):
        total = own.astype(F32)
        for d in range(1, count):
            total += received[(place + d) % count].astype(F32)
        return total

    def local_grads(h):
        q_h, da_h = q_ref[:, cols[h]], da[:, cols[h]]
        gq_out[:, cols[h]] = (scale * (dot(dsloc[h], k_ref[:, cols[h]]) + dot(dssum[h], sk[h]))).astype(BF16)
        dkl[h] = scale * dot(dsloc[h], q_h, TN)
        dvl[h] = dot(pbloc[h], da_h, TN)

    for h in range(heads):
        local_grads(h)

    for s in range(1, far - 1):
        relay(s)

    for h in range(heads):
        arrive(gk1(h), X)
        s2k[h] = gathered(kg[h, mx], rk.at[h], mx, X).astype(BF16)
    start(gk2, Z)
    for h in range(heads):
        arrive(gv1(h), Z)
        s2v[h] = gathered(vg[h, mz], rv.at[h], mz, Z).astype(BF16)
    start(gv2, X)

    if far > 1:
        relay(far - 1)

    for chunk in range(CHUNKS):
        place = slice(chunk * part, (chunk + 1) * part)
        value = ysum[my, place].astype(F32)
        for c, (which, way, hops) in enumerate(chains):
            if which == chunk:
                hop(c, hops - 1).wait_recv()
                value += ring[c, hops - 1].astype(F32)
        att_out[place, :] = value.astype(BF16)

    def spread(local, extra):
        shaped = local.reshape(blocks, SUMMARY, HEAD_DIM)
        return jnp.where(chosen, shaped + extra[None], shaped).reshape(rows, HEAD_DIM).astype(BF16)

    arrive(gk2, Z)
    sum_dk = gathered(s2k[:, mz], r2k, mz, Z)
    for h in range(heads):
        gk_out[:, cols[h]] = spread(dkl[h], sum_dk[h])
    arrive(gv2, X)
    sum_dv = gathered(s2v[:, mx], r2v, mx, X)
    for h in range(heads):
        gv_out[:, cols[h]] = spread(dvl[h], sum_dv[h])

    for make, count in ((ka, Z), (va, X), (gk2, Z), (gv2, X)):
        sent(make, count)
    for h in range(heads):
        for make, count in ((kb, X), (vb, Z), (gk1, X), (gv1, Z)):
            sent(make(h), count)

    @pl.loop(0, Y)
    def _(i):
        lend(i).wait_send()

    for h in range(heads):
        share(h).wait_send()

    for c, (chunk, way, hops) in enumerate(chains):
        for s in range(hops):
            hop(c, s).wait_send()


def store(*refs):
    sources, targets, sem = refs[:4], refs[4:8], refs[8]
    copies = [pltpu.make_async_copy(a, b, sem.at[i]) for i, (a, b) in enumerate(zip(sources, targets))]
    for c in copies:
        c.start()
    for c in copies:
        c.wait()


def on_device(sizes, queries, key_rows, value_rows, summary_index, out_weight, out_grad):
    X, Z, Y, C = sizes
    rows, width = queries.shape
    heads = width // HEAD_DIM
    slots = X * Z * SUMMARY
    N = Y * C
    vmem = pl.BlockSpec(memory_space=pltpu.VMEM)
    hbm = pl.BlockSpec(memory_space=pl.ANY)
    out = jax.ShapeDtypeStruct((rows, width), BF16)
    table = (heads, X, Z, SUMMARY, HEAD_DIM)
    across = (heads, Z, X, SUMMARY, HEAD_DIM)
    far = max(Y // 2, 1)
    scratch = [
        pltpu.SMEM((1,), jnp.int32),
        pltpu.VMEM((rows, width), BF16),
        pltpu.VMEM((rows, width), BF16),
        pltpu.VMEM((rows, width), BF16),
        pltpu.VMEM((N, width, width), BF16),
        pltpu.VMEM((N, rows, width), BF16),
        pltpu.VMEM(table, BF16),
        pltpu.VMEM(across, BF16),
        pltpu.VMEM((heads, slots, HEAD_DIM), BF16),
        pltpu.VMEM((rows, width), BF16),
        pltpu.VMEM((rows, 2 * width), BF16),
        pltpu.VMEM((heads, rows, rows), F32),
        pltpu.VMEM((heads, rows, rows), F32),
        pltpu.VMEM((heads, rows, rows), BF16),
        pltpu.VMEM((heads, rows, rows), BF16),
        pltpu.VMEM((heads, rows, slots), BF16),
        pltpu.VMEM((Y, width, width), BF16),
        pltpu.VMEM((Y, rows, width), BF16),
        pltpu.VMEM((2 * CHUNKS, far, rows // CHUNKS, width), BF16),
        pltpu.VMEM(table, BF16),
        pltpu.VMEM(across, BF16),
        pltpu.VMEM((heads, X, Z, SUMMARY, HEAD_DIM), BF16),
        pltpu.VMEM((heads, Z, X, SUMMARY, HEAD_DIM), BF16),
        pltpu.VMEM((heads, Z, SUMMARY, HEAD_DIM), BF16),
        pltpu.VMEM((heads, X, SUMMARY, HEAD_DIM), BF16),
        pltpu.VMEM((Z, heads, SUMMARY, HEAD_DIM), BF16),
        pltpu.VMEM((X, heads, SUMMARY, HEAD_DIM), BF16),
        pltpu.VMEM((heads, rows, HEAD_DIM), F32),
        pltpu.VMEM((heads, rows, HEAD_DIM), F32),
        pltpu.SemaphoreType.DMA((2, N)),
        pltpu.SemaphoreType.DMA((4,)),
        pltpu.SemaphoreType.DMA((4 + 4 * heads, max(X, Z))),
        pltpu.SemaphoreType.DMA((4 + 4 * heads, max(X, Z))),
        pltpu.SemaphoreType.DMA((Y + heads,)),
        pltpu.SemaphoreType.DMA((Y + heads,)),
        pltpu.SemaphoreType.DMA((2 * CHUNKS, far)),
        pltpu.SemaphoreType.DMA((2 * CHUNKS, far)),
    ]
    held = pltpu.VMEM((rows, width), BF16)
    results = pl.pallas_call(
        functools.partial(kernel, sizes),
        out_shape=(held, held, held, held),
        in_specs=[hbm] * 6,
        out_specs=(vmem, vmem, vmem, vmem),
        scratch_shapes=scratch,
        compiler_params=pltpu.CompilerParams(collective_id=0, has_side_effects=True),
        name="sparse_attention_step",
    )(summary_index, queries, key_rows, value_rows, out_weight, out_grad)
    return tuple(pl.pallas_call(
        store,
        out_shape=(out, out, out, out),
        in_specs=[vmem] * 4,
        out_specs=(hbm,) * 4,
        scratch_shapes=[pltpu.SemaphoreType.DMA((4,))],
        name="store_results",
    )(*[pltpu.with_memory_space_constraint(r, pltpu.VMEM) for r in results]))


def solution(mesh, sizes=SIZES):
    return jax.shard_map(
        functools.partial(on_device, sizes),
        mesh=mesh,
        in_specs=(
            P("ctx", "head"),
            P("ctx", "head"),
            P("ctx", "head"),
            P("ctx"),
            P("head", None),
            P("ctx", None),
        ),
        out_specs=(P("ctx", "head"), P("ctx", "head"), P("ctx", "head"), P("ctx", "head")),
        check_vma=False,
    )
```

time: 71.1 us -> 62.9 us (0.88)
  the two profiles are of different devices: /device:TPU:16 before, /device:TPU:32 now
where the time goes in v2:
time: 62.9 us; the launch traced here: 62.7 us
  Pallas kernels  61.4 us (98%)
  between operations  1.29 us (2%)
    pallas_call x1, Pallas kernels, on_device(): pl.pallas_call(functools.partial(kernel, sizes), out_shape=(held, held, h...  60.6 us

profile of v2, /device:TPU:32, one launch (start us, length us, event | category | flops | bytes accessed | tf_op | source)
XLA Modules:
  0.0 62.7 jit_solution(396084265800675429)
XLA Ops:
  1.3 60.6 %sparse_attention_step.1 = (bf16[128,384]{1,0:T(8,128)(2,1)S(1)}, bf16[128,384]{1,0:T(8,128)(2,1)S(1)}, bf16[128,384]{1,0:T(8,128)(2,1)S(1)}, bf16[128,384]{1,0:T(8,128)(2,1)S(1)}) custom-call(s32[1]{0:T(128)S(6)} %copy.10.idx_hbm, bf16[128,384]{1,0:T(8,128)(2,1)} %q_hbm.1, bf16[128,384]{1,0:T(8,128)(2,1)} %k_hbm.1, bf16[128,384]{1,0:T(8,128)(2,1)} %v_hbm.1, ...), custom_call_target="tpu_custom_call" | custom-call | tf_op jit(solution)/shard_map/sparse_attention_step/pallas_call | solution.py:399
  61.9 0.8 %store_results.1 = (bf16[128,384]{1,0:T(8,128)(2,1)}, bf16[128,384]{1,0:T(8,128)(2,1)}, bf16[128,384]{1,0:T(8,128)(2,1)}, bf16[128,384]{1,0:T(8,128)(2,1)}) custom-call(bf16[128,384]{1,0:T(8,128)(2,1)S(1)} %get-tuple-element.8.refs_0_, bf16[128,384]{1,0:T(8,128)(2,1)S(1)} %get-tuple-element.9.refs_1_, bf16[128,384]{1,0:T(8,128)(2,1)S(1)} %get-tuple-element.10.refs_2_, ...), custom_call_target="tpu_custom_call" | custom-call | tf_op jit(solution)/shard_map/store_results/pallas_call | solution.py:408

commit v3 on v2

--- a/solution.py
+++ b/solution.py
@@ -25,7 +25,7 @@
 
 def kernel(sizes, idx_hbm, q_hbm, k_hbm, v_hbm, w_hbm, og_hbm,
            att_out, gq_out, gk_out, gv_out,
-           idx_ref, q_ref, k_ref, v_ref, w_v, og_v, tk, tv, sk, da, attn, sloc, dploc, dsloc, pbloc, dssum,
+           idx_ref, q_ref, k_ref, v_ref, w_v, og_v, sums, tk, tv, sk, da, attn, sloc, dploc, dsloc, pbloc, dssum,
            w_p, ysum, ring, kg, vg, rk, rv, s2k, s2v, r2k, r2v, dkl, dvl,
            load_sem, in_sem, send_sem, recv_sem, psend_sem, precv_sem, rsend_sem, rrecv_sem):
     X, Z, Y, C = sizes
@@ -132,9 +132,9 @@
         return copy(s2v.at[:, (mx + d) % X], r2v.at[mx], GV2, d, at_x(d))
 
     def start(make, count):
-        @pl.loop(1, count)
-        def _(d):
-            make(d).start()
+        @pl.loop(0, count - 1)
+        def _(i):
+            make(count // 2 + ((i + 1) // 2) * (2 * (i % 2) - 1)).start()
 
     def arrive(make, count):
         @pl.loop(1, count)
@@ -164,18 +164,22 @@
     def _(i):
         lend(i).start()
 
-    total = jnp.zeros((rows, width), F32)
-    for n in range(N):
-        load_g(n).wait()
-        load_w(n).wait()
-        total += dot(og_v[n], w_v[n], NT)
-    da[...] = total.astype(BF16)
-
     arrive(ka, Z)
     start(kb(0), X)
     arrive(va, X)
     start(vb(0), Z)
     for h in range(1, heads):
+        if h == heads - 1:
+            sums[...] = jnp.zeros((rows, width), F32)
+
+            @pl.loop(0, N)
+            def _(n):
+                load_g(n).wait()
+                load_w(n).wait()
+                sums[...] += dot(og_v[n], w_v[n], NT)
+
+            da[...] = sums[...].astype(BF16)
+
         start(kb(h), X)
         start(vb(h), Z)
 
@@ -363,6 +367,7 @@
         pltpu.VMEM((rows, width), BF16),
         pltpu.VMEM((N, width, width), BF16),
         pltpu.VMEM((N, rows, width), BF16),
+        pltpu.VMEM((rows, width), F32),
         pltpu.VMEM(table, BF16),
         pltpu.VMEM(across, BF16),
         pltpu.VMEM((heads, slots, HEAD_DIM), BF16),

time: 62.9 us -> 60.8 us (0.967)
  the two profiles are of different devices: /device:TPU:32 before, /device:TPU:2 now
where the time goes in v3:
time: 60.8 us; the launch traced here: 60.6 us
  Pallas kernels  59.3 us (98%)
  between operations  1.29 us (2%)
    pallas_call x1, Pallas kernels, on_device(): pl.pallas_call(functools.partial(kernel, sizes), out_shape=(held, held, h...  58.6 us

profile of v3, /device:TPU:2, one launch (start us, length us, event | category | flops | bytes accessed | tf_op | source)
XLA Modules:
  0.0 60.6 jit_solution(2654461823559940829)
XLA Ops:
  1.3 58.6 %sparse_attention_step.1 = (bf16[128,384]{1,0:T(8,128)(2,1)S(1)}, bf16[128,384]{1,0:T(8,128)(2,1)S(1)}, bf16[128,384]{1,0:T(8,128)(2,1)S(1)}, bf16[128,384]{1,0:T(8,128)(2,1)S(1)}) custom-call(s32[1]{0:T(128)S(6)} %copy.10.idx_hbm, bf16[128,384]{1,0:T(8,128)(2,1)} %q_hbm.1, bf16[128,384]{1,0:T(8,128)(2,1)} %k_hbm.1, bf16[128,384]{1,0:T(8,128)(2,1)} %v_hbm.1, ...), custom_call_target="tpu_custom_call" | custom-call | tf_op jit(solution)/shard_map/sparse_attention_step/pallas_call | solution.py:404
  59.8 0.8 %store_results.1 = (bf16[128,384]{1,0:T(8,128)(2,1)}, bf16[128,384]{1,0:T(8,128)(2,1)}, bf16[128,384]{1,0:T(8,128)(2,1)}, bf16[128,384]{1,0:T(8,128)(2,1)}) custom-call(bf16[128,384]{1,0:T(8,128)(2,1)S(1)} %get-tuple-element.8.refs_0_, bf16[128,384]{1,0:T(8,128)(2,1)S(1)} %get-tuple-element.9.refs_1_, bf16[128,384]{1,0:T(8,128)(2,1)S(1)} %get-tuple-element.10.refs_2_, ...), custom_call_target="tpu_custom_call" | custom-call | tf_op jit(solution)/shard_map/store_results/pallas_call | solution.py:413
